TPU v7x, 32 devices: a whole 2x2x4 slice. The times are simulated.
32 devices in a mesh: grid: 8 (over z, y), tile: 4 (over x, core).
Axes of the slice: x: 2, y: 2, z: 4, core: 2. Of those that a mesh axis runs over, the one named last changes fastest.
Arguments:
- point_values: bfloat16 [256, 16384], P('grid', 'tile'), may hold values from -1.75 to 1.75
- sig_blocks: int32 [8, 16], P('grid'), may hold values from 0 to 31, as said below
- density: bfloat16 [16384, 16384], P('grid', 'tile'), may hold values from -0.0625 to 0.0625
- coulomb_core: bfloat16 [512, 512], replicated, may hold values from -0.25 to 0.25
- screen_mask: int32 [32, 32], replicated, may hold values 0 or 1
- ao_centers: float32 [3, 16384], replicated, may hold values from -1 to 1
- ao_widths: float32 [16384], replicated, may hold values from 0.25 to 1
- point_coords: float32 [3, 256], P(None, 'grid'), may hold values from -1 to 1
- lmo_coeffs: bfloat16 [16384, 1024], P('tile'), may hold values from -0.0625 to 0.0625
- domain_blocks: int32 [4, 16], replicated, may hold values from 0 to 31, as said below
Outputs:
- half: bfloat16 [1024, 16384], P('tile', 'grid')
Inputs may be any that keep to these rules, and one draw needn't show every extreme that they name: `sig_blocks`: each batch names 16 different AO blocks. `domain_blocks`: each strip's 16 blocks are different, and every AO block lies in the domain of some strip.
All inputs are finite; a program needn't handle non-finite values.
Results may differ from a plain program's by a relative error of at most 0.02.
Values may be sent and summed in bfloat16 or wider, within the bound.
A program may use at most 128 MiB of HBM per device.

v0:
```python
import jax
import jax.numpy as jnp
from jax import lax
from jax.sharding import PartitionSpec as P

highest = lax.Precision.HIGHEST


def kernel_weights(ao_centers, ao_widths, point_coords):
    offsets = ao_centers[:, None, :] - point_coords[:, :, None]
    return 1.0 / jnp.sqrt(jnp.sum(offsets * offsets, axis=0) + ao_widths[None, :])


def spread_mask(flag_rows, batch_points, block_size):
    batches, block_count = flag_rows.shape
    expanded = jnp.broadcast_to(
        flag_rows[:, None, :, None], (batches, batch_points, block_count, block_size)
    )
    return expanded.reshape(batches * batch_points, block_count * block_size)


def shards(
    point_values,
    sig_blocks,
    density,
    coulomb_core,
    screen_mask,
    ao_centers,
    ao_widths,
    point_coords,
    lmo_coeffs,
    domain_blocks,
):
    grid_count = lax.axis_size("grid")
    panel_index = lax.axis_index("tile")
    batches = sig_blocks.shape[0]
    own_rows, own_cols = density.shape
    points = point_values.shape[0]
    batch_points = points // batches
    block_size = coulomb_core.shape[0]
    total_aos = ao_widths.shape[0]
    all_blocks = total_aos // block_size
    col_blocks = own_cols // block_size
    row_blocks = own_rows // block_size
    block_ids = jnp.arange(all_blocks, dtype=jnp.int32)
    named_blocks = jnp.any(sig_blocks[:, :, None] == block_ids[None, None, :], axis=1).astype(
        jnp.float32
    )
    first_col = panel_index * col_blocks
    named_cols = lax.dynamic_slice_in_dim(named_blocks, first_col, col_blocks, 1)
    col_mask = spread_mask(named_cols, batch_points, block_size)
    masked_local = point_values * col_mask.astype(jnp.bfloat16)
    dest_named = jnp.max(named_blocks.reshape(batches, grid_count, row_blocks), axis=2)
    outgoing = masked_local.reshape(batches, batch_points, 1, own_cols) * dest_named[
        :, None, :, None
    ].astype(jnp.bfloat16)
    product = jnp.einsum(
        "bpgc,rc->bpgr",
        lax.all_to_all(outgoing, "grid", split_axis=2, concat_axis=2, tiled=True),
        density,
        preferred_element_type=jnp.float32,
    )
    arrivals = lax.all_to_all(
        product.astype(jnp.bfloat16), "grid", split_axis=2, concat_axis=2, tiled=True
    )
    row_mask = spread_mask(named_blocks, batch_points, block_size)
    partial_term = arrivals.reshape(points, total_aos).astype(jnp.float32) * row_mask
    coefficient = kernel_weights(ao_centers, ao_widths, point_coords)
    core_float = coulomb_core.astype(jnp.float32)
    screen_float = screen_mask.astype(jnp.float32)
    density_term = lax.psum(partial_term.astype(jnp.bfloat16), "tile").astype(jnp.float32)
    weighted = (coefficient * density_term).reshape(points, all_blocks, block_size)
    screen_rows = lax.dynamic_slice_in_dim(screen_float, first_col, col_blocks, 0)
    screened = jnp.einsum("kj,pja->pka", screen_rows, weighted, precision=highest)
    kernel_part = jnp.einsum(
        "ab,pkb->pka", core_float, screened, preferred_element_type=jnp.float32
    ).reshape(points, own_cols)
    coeff_cols = lax.dynamic_slice_in_dim(coefficient, panel_index * own_cols, own_cols, 1)
    potential = (coeff_cols * kernel_part * col_mask).astype(jnp.bfloat16)
    potential_out = jnp.broadcast_to(
        potential.reshape(batches, batch_points, 1, own_cols),
        (batches, batch_points, grid_count, own_cols),
    )
    whole_points = lax.all_gather(masked_local, "tile", axis=1, tiled=True)
    row_values, col_values = (
        lax.all_to_all(
            whole_points.reshape(batches, batch_points, grid_count, own_rows),
            "grid",
            split_axis=2,
            concat_axis=2,
            tiled=True,
        ),
        lax.all_to_all(potential_out, "grid", split_axis=2, concat_axis=2, tiled=True),
    )
    exch_tile = jnp.einsum(
        "bpgr,bpgc->rc", row_values, col_values, preferred_element_type=jnp.float32
    ).astype(jnp.bfloat16)
    number_of_slabs = domain_blocks.shape[0]
    localized_orbital_total = lmo_coeffs.shape[1]
    strip_width = localized_orbital_total // number_of_slabs
    local_ids = first_col + jnp.arange(col_blocks, dtype=jnp.int32)
    in_domain = jnp.any(domain_blocks[:, :, None] == local_ids[None, None, :], axis=1)
    domain_flags = jnp.transpose(in_domain)
    domain_mask = jnp.broadcast_to(
        domain_flags[:, None, :, None], (col_blocks, block_size, number_of_slabs, strip_width)
    ).reshape(own_cols, localized_orbital_total)
    region_expansion_factor = lmo_coeffs * domain_mask.astype(jnp.bfloat16)
    return lax.psum_scatter(
        lax.dot_general(
            region_expansion_factor,
            exch_tile,
            (((0,), (1,)), ((), ())),
            preferred_element_type=jnp.float32,
        ).astype(jnp.bfloat16),
        "tile",
        scatter_dimension=0,
        tiled=True,
    )


def solution(mesh):
    in_specs = (
        P("grid", "tile"),
        P("grid", None),
        P("grid", "tile"),
        P(),
        P(),
        P(),
        P(),
        P(None, "grid"),
        P("tile", None),
        P(),
    )
    out_specs = P("tile", "grid")
    return jax.shard_map(shards, mesh=mesh, in_specs=in_specs, out_specs=out_specs, check_vma=False)
```

profile of v0, /device:TPU:0, one launch (start us, length us, event | category | flops | bytes accessed | tf_op | source)
XLA Modules:
  0.0 288.2 jit_solution(9041671634119760462)
XLA Ops:
  6.5 0.8 fusion.26
  7.7 1.0 broadcast_multiply_fusion.1
  8.9 55.3 %all_to_all.20 = bf16[1,32,8,4096]{3,1,0,2:T(8,128)(2,1)S(1)} all-to-all(bf16[1,32,8,4096]{3,1,0,2:T(8,128)(2,1)S(1)} %broadcast_multiply_fusion), channel_id=1, replica_groups=mesh['grid'=8,'tile'=4] {'grid'}, dimensions={2} | all-to-all | bytes 4194304 | tf_op jit(solution)/shard_map/all_to_all | solution.py:59
  64.3 9.6 %fusion.11 = bf16[1,32,8,2048]{3,2,1,0:T(8,128)(2,1)} fusion(bf16[2048,4096]{1,0:T(8,128)(2,1)} %param.12, bf16[1,32,8,4096]{3,1,0,2:T(8,128)(2,1)S(1)} %all_to_all.20), kind=kOutput, calls=%fused_computation.9 | convolution fusion | flops 4295491584 | bytes 19922944 | tf_op jit(solution)/shard_map/bpgc,rc->bpgr/dot_general | solution.py:57
  73.8 2.8 copy.25
  76.6 3.6 %all-to-all-start.2 = ((bf16[1,32,8,2048]{3,1,0,2:T(8,128)(2,1)}), bf16[1,32,8,2048]{3,1,0,2:T(8,128)(2,1)S(1)}, u32[]{:S(2)}, u32[]{:S(2)}) async-start(bf16[1,32,8,2048]{3,1,0,2:T(8,128)(2,1)} %copy.25), calls=%async_computation.2 | async-start | bytes 2097152 | tf_op jit(solution)/shard_map/all_to_all | solution.py:63
  81.1 24.7 %all-to-all-done.2 = bf16[1,32,8,2048]{3,1,0,2:T(8,128)(2,1)S(1)} async-done(((bf16[1,32,8,2048]{3,1,0,2:T(8,128)(2,1)}), bf16[1,32,8,2048]{3,1,0,2:T(8,128)(2,1)S(1)}, u32[]{:S(2)}, u32[]{:S(2)}) %all-to-all-start.2) | async-done | bytes 1048608 | tf_op jit(solution)/shard_map/all_to_all | solution.py:63
  106.0 1.1 multiply_convert_fusion
  107.2 0.8 multiply_reduce_fusion
  108.0 1.8 copy.30
  109.9 1.6 copy.22
  111.5 4.2 %all-to-all-start = ((bf16[1,32,8,2048]{3,1,0,2:T(8,128)(2,1)}), bf16[1,32,8,2048]{3,1,0,2:T(8,128)(2,1)}, u32[]{:S(2)}, u32[]{:S(2)}) async-start(bf16[1,32,8,2048]{3,1,0,2:T(8,128)(2,1)} %copy.22), calls=%async_computation | async-start | bytes 2097152 | tf_op jit(solution)/shard_map/all_to_all | solution.py:86
  115.7 26.8 %all-reduce.2.cloned.1.call-done = bf16[32,16384]{1,0:T(8,128)(2,1)} async-done(((bf16[32,16384]{1,0:T(8,128)(2,1)}), bf16[32,16384]{1,0:T(8,128)(2,1)}) %all-reduce.2.cloned.1.call-update) | async-done | bytes 1048592 | tf_op jit(solution)/shard_map/psum | solution.py:71
  142.5 1.5 convert_multiply_fusion
  144.0 1.2 copy.33
  145.2 1.9 convolution_bitcast_fusion
  147.9 1.6 broadcast_in_dim.49
  149.5 5.9 %all-to-all-start.3 = ((bf16[1,32,8,4096]{3,1,0,2:T(8,128)(2,1)}), bf16[1,32,8,4096]{3,1,0,2:T(8,128)(2,1)S(1)}, u32[]{:S(2)}, u32[]{:S(2)}) async-start(bf16[1,32,8,4096]{3,1,0,2:T(8,128)(2,1)} %broadcast_in_dim.49), calls=%async_computation.3 | async-start | bytes 4194304 | tf_op jit(solution)/shard_map/all_to_all | solution.py:93
  156.0 2.2 broadcast_in_dim.18
  158.2 4.0 %copy.28 = pred[512,8,4,256]{3,1,2,0:T(8,128)(4,1)} copy(pred[512,8,4,256]{3,2,1,0:T(4,128)(4,1)S(1)} %bitcast.72) | data formatting | bytes 8388608
  162.3 40.5 %all-to-all-done.3 = bf16[1,32,8,4096]{3,1,0,2:T(8,128)(2,1)S(1)} async-done(((bf16[1,32,8,4096]{3,1,0,2:T(8,128)(2,1)}), bf16[1,32,8,4096]{3,1,0,2:T(8,128)(2,1)S(1)}, u32[]{:S(2)}, u32[]{:S(2)}) %all-to-all-start.3) | async-done | bytes 2097184 | tf_op jit(solution)/shard_map/all_to_all | solution.py:93
  202.8 10.0 %bitcast_convert_fusion.clone.7 = bf16[2048,4096]{1,0:T(8,128)(2,1)} fusion(bf16[1,32,8,4096]{3,1,0,2:T(8,128)(2,1)S(1)} %all-to-all-done.3, bf16[1,32,8,2048]{3,1,0,2:T(8,128)(2,1)} %all-to-all-done), kind=kOutput, calls=%fused_computation.clone.clone.clone.clone.clone.2 | convolution fusion | flops 4303355904 | bytes 19922944 | tf_op jit(solution)/shard_map/bpgr,bpgc->rc/dot_general | solution.py:95
  212.8 25.2 %fusion.5 = bf16[1024,2048]{1,0:T(8,128)(2,1)} fusion(pred[4096,1024]{1,0:T(8,128)(4,1)} %bitcast.77, bf16[4096,1024]{1,0:T(8,128)(2,1)} %param.18, bf16[2048,4096]{1,0:T(8,128)(2,1)} %bitcast_convert_fusion.clone.7), kind=kOutput, calls=%fused_computation.7 | convolution fusion | flops 17186160640 | bytes 33554432 | tf_op jit(solution)/shard_map/dot_general | solution.py:109
  237.9 43.7 %reduce-scatter.2.cloned.1.call-done = bf16[256,2048]{1,0:T(8,128)(2,1)} async-done(((bf16[1024,2048]{1,0:T(8,128)(2,1)}), bf16[256,2048]{1,0:T(8,128)(2,1)}) %reduce-scatter.2.cloned.1.call-update) | async-done | bytes 1048592 | tf_op jit(solution)/shard_map/reduce_scatter | solution.py:108
  (39 shorter events, 3.0 us)
Async XLA Ops:
  6.5 140.6 %copy-start = (bf16[512,512]{1,0:T(8,128)(2,1)S(1)}, bf16[512,512]{1,0:T(8,128)(2,1)}, u32[]{:S(2)}) copy-start(bf16[512,512]{1,0:T(8,128)(2,1)} %param.13) | copy-start | bytes 1572868
  8.7 55.6 %copy-start.2 = (bf16[32,4096]{1,0:T(8,128)(2,1)}, bf16[32,4096]{1,0:T(8,128)(2,1)S(1)}, u32[]{:S(2)}) copy-start(bf16[32,4096]{1,0:T(8,128)(2,1)S(1)} %broadcast_multiply_fusion.1) | copy-start | bytes 786436
  76.6 29.2 %all-to-all-start.2 = ((bf16[1,32,8,2048]{3,1,0,2:T(8,128)(2,1)}), bf16[1,32,8,2048]{3,1,0,2:T(8,128)(2,1)S(1)}, u32[]{:S(2)}, u32[]{:S(2)}) async-start(bf16[1,32,8,2048]{3,1,0,2:T(8,128)(2,1)} %copy.25), calls=%async_computation.2 | async-start | bytes 2097152 | tf_op jit(solution)/shard_map/all_to_all | solution.py:63
  80.2 27.8 %all-gather.2.cloned.1.call-start = ((), (), s32[]{:S(2)}) async-start(), calls=%async_computation.5 | async-start | bytes 1310720 | tf_op jit(solution)/shard_map/all_gather | solution.py:84
  80.9 61.6 %all-reduce.2.cloned.1.call-start = ((), (), s32[]{:S(2)}) async-start(), calls=%async_computation.6 | async-start | bytes 2097152 | tf_op jit(solution)/shard_map/psum | solution.py:71
  106.0 1.2 copy-start.3
  106.0 1.2 copy-start.6
  109.8 32.6 %copy-start.4 = (f32[16384]{0:T(1024)S(1)}, f32[16384]{0:T(1024)}, u32[]{:S(2)}) copy-start(f32[16384]{0:T(1024)} %param.16) | copy-start | bytes 196612
  111.5 36.4 %all-to-all-start = ((bf16[1,32,8,2048]{3,1,0,2:T(8,128)(2,1)}), bf16[1,32,8,2048]{3,1,0,2:T(8,128)(2,1)}, u32[]{:S(2)}, u32[]{:S(2)}) async-start(bf16[1,32,8,2048]{3,1,0,2:T(8,128)(2,1)} %copy.22), calls=%async_computation | async-start | bytes 2097152 | tf_op jit(solution)/shard_map/all_to_all | solution.py:86
  149.5 6.2 %copy-start.5 = (s32[4,16]{1,0:T(4,128)S(1)}, s32[4,16]{1,0:T(4,128)}, u32[]{:S(2)}) copy-start(s32[4,16]{1,0:T(4,128)} %param.19) | copy-start | bytes 772
  149.5 53.3 %all-to-all-start.3 = ((bf16[1,32,8,4096]{3,1,0,2:T(8,128)(2,1)}), bf16[1,32,8,4096]{3,1,0,2:T(8,128)(2,1)S(1)}, u32[]{:S(2)}, u32[]{:S(2)}) async-start(bf16[1,32,8,4096]{3,1,0,2:T(8,128)(2,1)} %broadcast_in_dim.49), calls=%async_computation.3 | async-start | bytes 4194304 | tf_op jit(solution)/shard_map/all_to_all | solution.py:93
  155.4 126.2 %reduce-scatter.2.cloned.1.call-start = ((), (), s32[]{:S(2)}) async-start(), calls=%async_computation.7 | async-start | bytes 5242880 | tf_op jit(solution)/shard_map/reduce_scatter | solution.py:108
  237.9 43.7 %copy-start.1 = (bf16[512,512]{1,0:T(8,128)(2,1)S(1)}, bf16[512,512]{1,0:T(8,128)(2,1)}, u32[]{:S(2)}) copy-start(bf16[512,512]{1,0:T(8,128)(2,1)} %param.13) | copy-start | bytes 1572868
Sparse Core Ops, SparseCore 0:
  82.6 18.0 all-gather.1
  107.3 35.1 all-reduce.1
  238.1 43.5 reduce-scatter.1
where the time goes:
time: 289 us; the launch traced here: 288 us
  waiting for transfers between devices  136 us (47%)
  blocking collectives  55.3 us (19%)
  matrix products  46.9 us (16%)
  local copies, waits for them, and re-layouts  16.3 us (6%)
  starting transfers between devices  14 us (5%)
  between operations  13.3 us (5%)
  other arithmetic  5.85 us (2%)
    all_to_all x1, blocking collectives, shards(): lax.all_to_all(outgoing, 'grid', split_axis=2, concat_axis=2, tiled=True)  55.3 us
    reduce_scatter x1, waiting for transfers between devices, shards(): lax.psum_scatter(lax.dot_general(region_expansion_factor, exch_tile, (((0...  43.7 us
    all_to_all x1, waiting for transfers between devices, shards(): lax.all_to_all(potential_out, 'grid', split_axis=2, concat_axis=2, tiled=...  40.5 us
    psum x1, waiting for transfers between devices, shards(): lax.psum(partial_term.astype(jnp.bfloat16), 'tile').astype(jnp.float32)  26.8 us
    dot_general x1, matrix products, shards(): lax.dot_general(region_expansion_factor, exch_tile, (((0,), (1,)), ((), (...  25.2 us
    all_to_all x1, waiting for transfers between devices, shards(): lax.all_to_all(product.astype(jnp.bfloat16), 'grid', split_axis=2, concat...  24.7 us
    dot_general x1, matrix products, shards(): jnp.einsum('bpgr,bpgc->rc', row_values, col_values, preferred_element_typ...  9.96 us
    dot_general x1, matrix products, shards(): jnp.einsum('bpgc,rc->bpgr', lax.all_to_all(outgoing, 'grid', split_axis=2...  9.56 us
  transfers between devices with their start and end apart: 6, of which 4 were waited for; matrix products, arithmetic and copies ran while one was open for 6% of the time, Pallas kernels for 0%

commit v1 on v0

--- a/solution.py
+++ b/solution.py
@@ -4,6 +4,12 @@
 from jax.sharding import PartitionSpec as P
 
 highest = lax.Precision.HIGHEST
+
+
+def add_all(block, mesh_axis):
+    pieces = lax.all_gather(block, mesh_axis, axis=0, tiled=False)
+    total = pieces.sum(axis=0)
+    return total
 
 
 def kernel_weights(ao_centers, ao_widths, point_coords):
@@ -68,7 +74,7 @@
     coefficient = kernel_weights(ao_centers, ao_widths, point_coords)
     core_float = coulomb_core.astype(jnp.float32)
     screen_float = screen_mask.astype(jnp.float32)
-    density_term = lax.psum(partial_term.astype(jnp.bfloat16), "tile").astype(jnp.float32)
+    density_term = add_all(partial_term.astype(jnp.bfloat16), "tile").astype(jnp.float32)
     weighted = (coefficient * density_term).reshape(points, all_blocks, block_size)
     screen_rows = lax.dynamic_slice_in_dim(screen_float, first_col, col_blocks, 0)
     screened = jnp.einsum("kj,pja->pka", screen_rows, weighted, precision=highest)

time: 289 us -> 291 us (level)
  other arithmetic: 5.85 us -> 9.32 us
  local copies, waits for them, and re-layouts: 16.3 us -> 19.5 us
  waiting for transfers between devices: 136 us -> 133 us
    psum x1 -> x0, waiting for transfers between devices: 26.8 us -> none  [shards(): lax.psum(partial_term.astype(jnp.bfloat16), 'tile').astype(jnp.float32)]
    all_gather x0 -> x1, waiting for transfers between devices: none -> 22.3 us  [add_all(): pieces = lax.all_gather(block, mesh_axis, axis=0, tiled=False)]
    reduce_sum x0 -> x1, other arithmetic: none -> 4.15 us  [add_all(): total = pieces.sum(axis=0)]
    unnamed x23 -> x25, local copies, waits for them, and re-layouts: 7.83 us -> 10.8 us
  transfers between devices with their start and end apart: 6 -> 6, of which waited for: 4 -> 4; matrix products, arithmetic and copies ran while one was open for 6% -> 8% of each run, Pallas kernels for 0% -> 0%
where the time goes in v1:
time: 291 us
  waiting for transfers between devices  133 us (46%)
  blocking collectives  55.3 us (19%)
  matrix products  46.9 us (16%)
  local copies, waits for them, and re-layouts  19.5 us (7%)
  starting transfers between devices  13.8 us (5%)
  between operations  13.3 us (5%)
  other arithmetic  9.32 us (3%)
    all_to_all x1, blocking collectives, shards(): lax.all_to_all(outgoing, 'grid', split_axis=2, concat_axis=2, tiled=True)  55.3 us
    reduce_scatter x1, waiting for transfers between devices, shards(): lax.psum_scatter(lax.dot_general(region_expansion_factor, exch_tile, (((0...  42.9 us
    all_to_all x1, waiting for transfers between devices, shards(): lax.all_to_all(potential_out, 'grid', split_axis=2, concat_axis=2, tiled=...  42 us
    dot_general x1, matrix products, shards(): lax.dot_general(region_expansion_factor, exch_tile, (((0,), (1,)), ((), (...  25.2 us
    all_to_all x1, waiting for transfers between devices, shards(): lax.all_to_all(product.astype(jnp.bfloat16), 'grid', split_axis=2, concat...  24.7 us
    all_gather x1, waiting for transfers between devices, add_all(): pieces = lax.all_gather(block, mesh_axis, axis=0, tiled=False)  22.3 us
    unnamed x25, local copies, waits for them, and re-layouts  10.8 us
    dot_general x1, matrix products, shards(): jnp.einsum('bpgr,bpgc->rc', row_values, col_values, preferred_element_typ...  10 us
  transfers between devices with their start and end apart: 6, of which 4 were waited for; matrix products, arithmetic and copies ran while one was open for 8% of the time, Pallas kernels for 0%

profile of v1, /device:TPU:0, one launch (start us, length us, event | category | flops | bytes accessed | tf_op | source)
XLA Modules:
  0.0 290.7 jit_solution(5526961850751369359)
XLA Ops:
  6.5 0.8 fusion.31
  7.7 1.0 broadcast_multiply_fusion.1
  8.9 55.3 %all_to_all.20 = bf16[1,32,8,4096]{3,1,0,2:T(8,128)(2,1)S(1)} all-to-all(bf16[1,32,8,4096]{3,1,0,2:T(8,128)(2,1)S(1)} %broadcast_multiply_fusion), channel_id=1, replica_groups=mesh['grid'=8,'tile'=4] {'grid'}, dimensions={2} | all-to-all | bytes 4194304 | tf_op jit(solution)/shard_map/all_to_all | solution.py:65
  64.3 9.6 %fusion.11 = bf16[1,32,8,2048]{3,2,1,0:T(8,128)(2,1)} fusion(bf16[2048,4096]{1,0:T(8,128)(2,1)} %param.12, bf16[1,32,8,4096]{3,1,0,2:T(8,128)(2,1)S(1)} %all_to_all.20), kind=kOutput, calls=%fused_computation.9 | convolution fusion | flops 4295491584 | bytes 19922944 | tf_op jit(solution)/shard_map/bpgc,rc->bpgr/dot_general | solution.py:63
  73.8 2.8 copy.25
  76.6 3.6 %all-to-all-start.2 = ((bf16[1,32,8,2048]{3,1,0,2:T(8,128)(2,1)}), bf16[1,32,8,2048]{3,1,0,2:T(8,128)(2,1)S(1)}, u32[]{:S(2)}, u32[]{:S(2)}) async-start(bf16[1,32,8,2048]{3,1,0,2:T(8,128)(2,1)} %copy.25), calls=%async_computation.2 | async-start | bytes 2097152 | tf_op jit(solution)/shard_map/all_to_all | solution.py:69
  81.1 24.7 %all-to-all-done.2 = bf16[1,32,8,2048]{3,1,0,2:T(8,128)(2,1)S(1)} async-done(((bf16[1,32,8,2048]{3,1,0,2:T(8,128)(2,1)}), bf16[1,32,8,2048]{3,1,0,2:T(8,128)(2,1)S(1)}, u32[]{:S(2)}, u32[]{:S(2)}) %all-to-all-start.2) | async-done | bytes 1048608 | tf_op jit(solution)/shard_map/all_to_all | solution.py:69
  106.3 1.1 multiply_convert_fusion
  108.3 2.5 copy.32
  110.8 1.8 copy.31
  112.6 1.6 copy.22
  114.2 4.4 %all-to-all-start = ((bf16[1,32,8,2048]{3,1,0,2:T(8,128)(2,1)}), bf16[1,32,8,2048]{3,1,0,2:T(8,128)(2,1)}, u32[]{:S(2)}, u32[]{:S(2)}) async-start(bf16[1,32,8,2048]{3,1,0,2:T(8,128)(2,1)} %copy.22), calls=%async_computation | async-start | bytes 2097152 | tf_op jit(solution)/shard_map/all_to_all | solution.py:92
  118.6 22.3 %all-gather.5.cloned.1.call-done = bf16[4,32,16384]{2,1,0:T(8,128)(2,1)} async-done(((bf16[1,32,16384]{2,1,0:T(8,128)(2,1)}), bf16[4,32,16384]{2,1,0:T(8,128)(2,1)}) %all-gather.5.cloned.1.call-update) | async-done | bytes 4194320 | tf_op jit(solution)/shard_map/all_gather | solution.py:10
  140.9 4.2 %reduce_sum.25 = bf16[32,16384]{1,0:T(8,128)(2,1)} reduce(bf16[4,32,16384]{2,1,0:T(8,128)(2,1)} %all-gather.5.cloned.1.call-done, bf16[]{:T(256)} %constant.5.clone.1), dimensions={0}, to_apply=%region_4.0 | reduce | flops 1572864 | bytes 5242882 | tf_op jit(solution)/shard_map/reduce_sum | solution.py:11
  145.0 1.7 copy.34
  147.5 1.9 convolution_bitcast_fusion
  150.2 1.6 broadcast_in_dim.49
  151.8 5.6 %all-to-all-start.3 = ((bf16[1,32,8,4096]{3,1,0,2:T(8,128)(2,1)}), bf16[1,32,8,4096]{3,1,0,2:T(8,128)(2,1)S(1)}, u32[]{:S(2)}, u32[]{:S(2)}) async-start(bf16[1,32,8,4096]{3,1,0,2:T(8,128)(2,1)} %broadcast_in_dim.49), calls=%async_computation.3 | async-start | bytes 4194304 | tf_op jit(solution)/shard_map/all_to_all | solution.py:99
  157.9 2.2 broadcast_in_dim.18
  160.1 4.1 %copy.29 = pred[512,8,4,256]{3,1,2,0:T(8,128)(4,1)} copy(pred[512,8,4,256]{3,2,1,0:T(4,128)(4,1)S(1)} %bitcast.79) | data formatting | bytes 8388608
  164.2 42.0 %all-to-all-done.3 = bf16[1,32,8,4096]{3,1,0,2:T(8,128)(2,1)S(1)} async-done(((bf16[1,32,8,4096]{3,1,0,2:T(8,128)(2,1)}), bf16[1,32,8,4096]{3,1,0,2:T(8,128)(2,1)S(1)}, u32[]{:S(2)}, u32[]{:S(2)}) %all-to-all-start.3) | async-done | bytes 2097184 | tf_op jit(solution)/shard_map/all_to_all | solution.py:99
  206.1 10.0 %bitcast_convert_fusion.clone.7 = bf16[2048,4096]{1,0:T(8,128)(2,1)} fusion(bf16[1,32,8,4096]{3,1,0,2:T(8,128)(2,1)S(1)} %all-to-all-done.3, bf16[1,32,8,2048]{3,1,0,2:T(8,128)(2,1)} %all-to-all-done), kind=kOutput, calls=%fused_computation.clone.clone.clone.clone.clone.2 | convolution fusion | flops 4303355904 | bytes 19922944 | tf_op jit(solution)/shard_map/bpgr,bpgc->rc/dot_general | solution.py:101
  216.1 25.2 %fusion.5 = bf16[1024,2048]{1,0:T(8,128)(2,1)} fusion(pred[4096,1024]{1,0:T(8,128)(4,1)} %bitcast.82, bf16[4096,1024]{1,0:T(8,128)(2,1)} %param.18, bf16[2048,4096]{1,0:T(8,128)(2,1)} %bitcast_convert_fusion.clone.7), kind=kOutput, calls=%fused_computation.7 | convolution fusion | flops 17186160640 | bytes 33554432 | tf_op jit(solution)/shard_map/dot_general | solution.py:115
  241.3 42.9 %reduce-scatter.2.cloned.1.call-done = bf16[256,2048]{1,0:T(8,128)(2,1)} async-done(((bf16[1024,2048]{1,0:T(8,128)(2,1)}), bf16[256,2048]{1,0:T(8,128)(2,1)}) %reduce-scatter.2.cloned.1.call-update) | async-done | bytes 1048592 | tf_op jit(solution)/shard_map/reduce_scatter | solution.py:114
  (47 shorter events, 4.6 us)
Async XLA Ops:
  6.5 142.9 %copy-start = (bf16[512,512]{1,0:T(8,128)(2,1)S(1)}, bf16[512,512]{1,0:T(8,128)(2,1)}, u32[]{:S(2)}) copy-start(bf16[512,512]{1,0:T(8,128)(2,1)} %param.13) | copy-start | bytes 1572868
  8.7 55.6 %copy-start.3 = (bf16[32,4096]{1,0:T(8,128)(2,1)}, bf16[32,4096]{1,0:T(8,128)(2,1)S(1)}, u32[]{:S(2)}) copy-start(bf16[32,4096]{1,0:T(8,128)(2,1)S(1)} %broadcast_multiply_fusion.1) | copy-start | bytes 786436
  76.6 29.2 %all-to-all-start.2 = ((bf16[1,32,8,2048]{3,1,0,2:T(8,128)(2,1)}), bf16[1,32,8,2048]{3,1,0,2:T(8,128)(2,1)S(1)}, u32[]{:S(2)}, u32[]{:S(2)}) async-start(bf16[1,32,8,2048]{3,1,0,2:T(8,128)(2,1)} %copy.25), calls=%async_computation.2 | async-start | bytes 2097152 | tf_op jit(solution)/shard_map/all_to_all | solution.py:69
  80.2 30.6 %all-gather.3.cloned.1.call-start = ((), (), s32[]{:S(2)}) async-start(), calls=%async_computation.5 | async-start | bytes 1310720 | tf_op jit(solution)/shard_map/all_gather | solution.py:90
  80.9 60.0 %all-gather.5.cloned.1.call-start = ((), (), s32[]{:S(2)}) async-start(), calls=%async_computation.6 | async-start | bytes 5242880 | tf_op jit(solution)/shard_map/all_gather | solution.py:10
  106.2 1.2 copy-start.5
  106.2 1.2 copy-start.4
  106.3 1.2 copy-start.7
  114.2 36.0 %all-to-all-start = ((bf16[1,32,8,2048]{3,1,0,2:T(8,128)(2,1)}), bf16[1,32,8,2048]{3,1,0,2:T(8,128)(2,1)}, u32[]{:S(2)}, u32[]{:S(2)}) async-start(bf16[1,32,8,2048]{3,1,0,2:T(8,128)(2,1)} %copy.22), calls=%async_computation | async-start | bytes 2097152 | tf_op jit(solution)/shard_map/all_to_all | solution.py:92
  145.0 1.9 copy-start.2
  147.5 2.6 dynamic-slice-start
  151.8 5.7 %copy-start.6 = (s32[4,16]{1,0:T(4,128)S(1)}, s32[4,16]{1,0:T(4,128)}, u32[]{:S(2)}) copy-start(s32[4,16]{1,0:T(4,128)} %param.19) | copy-start | bytes 772
  151.8 54.3 %all-to-all-start.3 = ((bf16[1,32,8,4096]{3,1,0,2:T(8,128)(2,1)}), bf16[1,32,8,4096]{3,1,0,2:T(8,128)(2,1)S(1)}, u32[]{:S(2)}, u32[]{:S(2)}) async-start(bf16[1,32,8,4096]{3,1,0,2:T(8,128)(2,1)} %broadcast_in_dim.49), calls=%async_computation.3 | async-start | bytes 4194304 | tf_op jit(solution)/shard_map/all_to_all | solution.py:99
  157.5 126.7 %reduce-scatter.2.cloned.1.call-start = ((), (), s32[]{:S(2)}) async-start(), calls=%async_computation.7 | async-start | bytes 5242880 | tf_op jit(solution)/shard_map/reduce_scatter | solution.py:114
  241.3 42.9 %copy-start.1 = (bf16[512,512]{1,0:T(8,128)(2,1)S(1)}, bf16[512,512]{1,0:T(8,128)(2,1)}, u32[]{:S(2)}) copy-start(bf16[512,512]{1,0:T(8,128)(2,1)} %param.13) | copy-start | bytes 1572868
Sparse Core Ops, SparseCore 0:
  82.6 18.0 all-gather.2
  107.5 33.2 all-gather.4
  241.4 42.7 reduce-scatter.1
